TPU v7x, 512 devices: a whole 4x4x16 slice. The times are simulated.
512 devices in a mesh: lat: 4 (over x_hi, core), lon: 32 (over z, x_lo), tensor: 4 (over y).
Axes of the slice: x: 4 (x_hi: 2, x_lo: 2; x = x_hi * 2 + x_lo), y: 4, z: 16, core: 2. Of those that a mesh axis runs over, the one named last changes fastest.
Arguments:
- fields: bfloat16 [64, 768, 256], P('lat', 'lon'), may hold values from -8 to 8
- norm_gain1: float32 [256], replicated, may hold values from 0.5 to 1.5
- w_qkv: bfloat16 [256, 3, 8, 32], P(None, None, 'tensor'), may hold values from -0.1875 to 0.1875
- logit_scale: float32 [8], P('tensor'), may hold values from 1 to 64
- w_out: bfloat16 [8, 32, 256], P('tensor'), may hold values from -0.375 to 0.375
- attn_keep: int32 [64, 256], P('lat'), may hold values 0 or 1
- dw_kernel: bfloat16 [7, 7, 256], replicated, may hold values from -0.875 to 0.875
- norm_gain2: float32 [256], replicated, may hold values from 0.5 to 1.5
- w_up: bfloat16 [256, 1024], P(None, 'tensor'), may hold values from -0.375 to 0.375
- w_down: bfloat16 [1024, 256], P('tensor'), may hold values from -0.1875 to 0.1875
- mlp_keep: int32 [64, 256], P('lat'), may hold values 0 or 1
Outputs:
- result: bfloat16 [64, 768, 256], P('lat', 'lon')
All inputs are finite; a program needn't handle non-finite values. No bound on the sum of `attn_keep` or of `mlp_keep` on one device may be relied on, other than what follows from the above.
Results may differ from a plain program's by a relative error of at most 0.014.
Values may be sent and summed in bfloat16 or wider, within the bound.
A program may use at most 64 MiB of HBM per device.

v0:
```python
import math
import jax
import jax.numpy as jnp
from jax import lax
from jax.sharding import PartitionSpec as P

ln_eps = 1e-05
keep_prob = 0.9


def padded(shard, sides, width, wrap):
    for axis, dim in sides:
        size, length = (lax.axis_size(axis), shard.shape[dim])
        up = [(i, (i + 1) % size) for i in range(size if wrap else size - 1)]
        down = [(j, i) for i, j in up]
        last = lax.slice_in_dim(shard, length - width, length, axis=dim)
        first = lax.slice_in_dim(shard, 0, width, axis=dim)
        before = lax.ppermute(last, axis, up)
        after = lax.ppermute(first, axis, down)
        shard = jnp.concatenate([before, shard, after], axis=dim)
    return shard


def layer_norm(values, gain):
    widened = values.astype(jnp.float32)
    center = jnp.mean(widened, axis=-1, keepdims=True)
    spread = jnp.mean(jnp.square(widened - center), axis=-1, keepdims=True)
    return (widened - center) * lax.rsqrt(spread + ln_eps) * gain


def depthwise(wide, kernel, rows, cols):
    kernel_f = kernel.astype(jnp.float32)
    wide_f = wide.astype(jnp.float32)
    width = kernel.shape[0]
    total = jnp.zeros((rows, cols, wide.shape[2]), jnp.float32)
    for row_off in range(width):
        for col_off in range(width):
            total = (
                total
                + kernel_f[row_off, col_off]
                * wide_f[row_off : row_off + rows, col_off : col_off + cols]
            )
    return total


def widen(stream, margin):
    rows_wide = padded(stream, (("lat", 0),), margin, False)
    return padded(rows_wide, (("lon", 1),), margin, True)


def feed_forward(spatial, norm_gain2, w_up, w_down):
    normed2 = layer_norm(spatial, norm_gain2).astype(jnp.bfloat16)
    hidden = jax.nn.gelu(
        jnp.einsum("rlc,cf->rlf", normed2, w_up, preferred_element_type=jnp.float32),
        approximate=False,
    ).astype(jnp.bfloat16)
    return jnp.einsum("rlf,fc->rlc", hidden, w_down, preferred_element_type=jnp.float32)


def shards(
    fields,
    norm_gain1,
    w_qkv,
    logit_scale,
    w_out,
    attn_keep,
    dw_kernel,
    norm_gain2,
    w_up,
    w_down,
    mlp_keep,
):
    lat_rows, lon_cols, channels = fields.shape
    local_heads = w_qkv.shape[2]
    head_size = w_qkv.shape[3]
    logit_coef = logit_scale * (1.0 / math.sqrt(head_size))
    normed = layer_norm(fields, norm_gain1).astype(jnp.bfloat16)
    projected = jnp.einsum(
        "rlc,cjhd->rljhd", normed, w_qkv, preferred_element_type=jnp.float32
    ).astype(jnp.bfloat16)
    queries = projected[:, :, 0]
    keys_values = projected[:, :, 1:].reshape(lat_rows, lon_cols, 2 * local_heads * head_size)
    piece = lax.all_gather(keys_values, "lon", axis=1, tiled=True)
    running_max = jnp.full((lat_rows, local_heads, lon_cols), -1e30, jnp.float32)
    count = piece.shape[1]
    split_piece = piece.reshape(lat_rows, count, 2, local_heads, head_size)
    scores = jnp.einsum(
        "rqhd,rkhd->rhqk", queries, split_piece[:, :, 0], preferred_element_type=jnp.float32
    )
    scores = scores * logit_coef[None, :, None, None]
    new_max = jnp.maximum(running_max, jnp.max(scores, axis=-1))
    weights = jnp.exp(scores - new_max[..., None])
    new_sum = jnp.sum(weights, axis=-1)
    gathered = jnp.einsum(
        "rhqk,rkhd->rhqd",
        weights.astype(jnp.bfloat16),
        split_piece[:, :, 1],
        preferred_element_type=jnp.float32,
    )
    mixed = (gathered / new_sum[..., None]).astype(jnp.bfloat16)
    partial_value = jnp.einsum("rhqd,hdc->rqc", mixed, w_out, preferred_element_type=jnp.float32)
    attended = lax.psum(partial_value.astype(jnp.bfloat16), "tensor").astype(jnp.float32)
    attn_factor = (attn_keep.astype(jnp.float32) / keep_prob)[:, None, :]
    mlp_factor = (mlp_keep.astype(jnp.float32) / keep_prob)[:, None, :]
    margin = dw_kernel.shape[0] // 2
    stream = (fields.astype(jnp.float32) + attended * attn_factor).astype(jnp.bfloat16)
    spatial = depthwise(widen(stream, margin), dw_kernel, lat_rows, lon_cols).astype(jnp.bfloat16)
    ffn_sum = lax.psum(
        feed_forward(spatial, norm_gain2, w_up, w_down).astype(jnp.bfloat16), "tensor"
    ).astype(jnp.float32)
    result = (stream.astype(jnp.float32) + ffn_sum * mlp_factor).astype(jnp.bfloat16)
    return result


def solution(mesh):
    placed = (
        P("lat", "lon", None),
        P(),
        P(None, None, "tensor", None),
        P("tensor"),
        P("tensor", None, None),
        P("lat", None),
        P(),
        P(),
        P(None, "tensor"),
        P("tensor", None),
        P("lat", None),
    )
    return jax.shard_map(
        shards, mesh=mesh, in_specs=placed, out_specs=P("lat", "lon", None), check_vma=False
    )
```

profile of v0, /device:TPU:2, one launch (start us, length us, event | category | flops | bytes accessed | tf_op | source)
XLA Modules:
  0.0 309.6 jit_solution(4489916328786344057)
XLA Ops:
  6.5 1.1 convert_reduce_fusion
  7.7 1.2 fusion.18
  8.8 1.4 convolution_convert_fusion
  10.3 0.3 copy.12
  10.6 0.9 reshape.39
  11.5 0.0 all-gather.2.cloned.1.call-update
  11.5 0.0 all-reduce.3.cloned.1.call-start
  11.6 140.8 %all-gather.2.cloned.1.call-done = bf16[16,768,128]{2,1,0:T(8,128)(2,1)} async-done(((bf16[16,24,128]{2,1,0:T(8,128)(2,1)}), bf16[16,768,128]{2,1,0:T(8,128)(2,1)}) %all-gather.2.cloned.1.call-update) | async-done | bytes 3145744 | tf_op jit(solution)/shard_map/all_gather | solution.py:83
  152.4 4.7 %copy.13 = bf16[16,768,128]{1,2,0:T(8,128)(2,1)} copy(bf16[16,768,128]{2,1,0:T(8,128)(2,1)} %all-gather.2.cloned.1.call-done) | data formatting | bytes 6291456 | tf_op jit(solution)/shard_map/all_gather | solution.py:83
  157.1 2.0 multiply_reduce_fusion
  159.0 0.6 fusion
  159.7 0.0 copy-start.2
  159.7 0.0 copy-start.1
  159.7 3.2 %fusion.11 = bf16[16,24,256]{2,1,0:T(8,128)(2,1)} fusion(bf16[16,768,2,2,32]{1,4,3,2,0:T(8,128)(2,1)} %bitcast.96, f32[16,2,24,768]{3,2,1,0:T(8,128)S(1)} %get-tuple-element.63, f32[16,2,24]{2,1,0:T(2,128)S(1)} %broadcast_maximum_fusion, f32[2]{0:T(128)S(1)} %broadcast_multiply_fusion.2, f32[16,2,24]{2,1,0:T(2,128)S(1)} %fusion, ...), kind=kOutput, calls=%fused_computation.14 | convolution fusion | flops 52248576 | bytes 4167688 | tf_op jit(solution)/shard_map/rhqd,hdc->rqc/dot_general | solution.py:101
  162.9 0.0 all-reduce.3.cloned.1.call-update
  162.9 0.0 all-reduce.5.cloned.1.call-start
  163.0 54.8 %all-reduce.3.cloned.1.call-done = bf16[16,24,256]{2,1,0:T(8,128)(2,1)} async-done(((bf16[16,24,256]{2,1,0:T(8,128)(2,1)}), bf16[16,24,256]{2,1,0:T(8,128)(2,1)}) %all-reduce.3.cloned.1.call-update) | async-done | bytes 196624 | tf_op jit(solution)/shard_map/psum | solution.py:102
  217.8 1.0 fusion.24
  218.8 1.3 collective-permute-start
  220.1 1.3 collective-permute-start.1
  221.5 4.1 %collective-permute-done.1 = bf16[3,24,256]{2,1,0:T(8,128)(2,1)S(1)} collective-permute-done((bf16[3,24,256]{2,1,0:T(8,128)(2,1)S(1)}, bf16[3,24,256]{2,1,0:T(8,128)(2,1)S(1)}, u32[]{:S(2)}, u32[]{:S(2)}) %collective-permute-start.1) | collective-permute-done | bytes 36896 | tf_op jit(solution)/shard_map/ppermute | solution.py:19
  225.6 4.4 %collective-permute-start.2 = (bf16[22,3,256]{2,1,0:T(4,128)(2,1)S(1)}, bf16[22,3,256]{2,1,0:T(4,128)(2,1)S(1)}, u32[]{:S(2)}, u32[]{:S(2)}) collective-permute-start(bf16[22,3,256]{2,1,0:T(4,128)(2,1)S(1)} %get-tuple-element.9), channel_id=1, source_target_pairs={{0,4},{4,8},{8,12},{12,16},{16,20},{20,24},{24,28},{28,32},{32,36}... | collective-permute-start | bytes 101384 | tf_op jit(solution)/shard_map/ppermute | solution.py:18
  230.0 1.9 collective-permute-start.3
  231.9 4.9 %collective-permute-done.3 = bf16[22,3,256]{2,1,0:T(4,128)(2,1)S(1)} collective-permute-done((bf16[22,3,256]{2,1,0:T(4,128)(2,1)S(1)}, bf16[22,3,256]{2,1,0:T(4,128)(2,1)S(1)}, u32[]{:S(2)}, u32[]{:S(2)}) %collective-permute-start.3) | collective-permute-done | bytes 33824 | tf_op jit(solution)/shard_map/ppermute | solution.py:19
  236.8 0.1 maximum_convert_fusion
  237.0 2.9 convert_reduce_fusion.1
  239.9 0.2 fusion.21
  240.2 0.3 fusion.95
  240.5 1.8 convolution_convert_fusion.1
  242.3 0.0 all-reduce.5.cloned.1.call-update
  242.3 59.0 %all-reduce.5.cloned.1.call-done = bf16[16,24,256]{2,1,0:T(8,128)(2,1)} async-done(((bf16[16,24,256]{2,1,0:T(8,128)(2,1)}), bf16[16,24,256]{2,1,0:T(8,128)(2,1)}) %all-reduce.5.cloned.1.call-update) | async-done | bytes 196624 | tf_op jit(solution)/shard_map/psum | solution.py:108
  301.4 1.7 add_convert_fusion
  (33 shorter events, 0.2 us)
Async XLA Ops:
  6.5 233.6 %copy-start = (bf16[256,256]{1,0:T(8,128)(2,1)S(1)}, bf16[256,256]{1,0:T(8,128)(2,1)}, u32[]{:S(2)}) copy-start(bf16[256,256]{1,0:T(8,128)(2,1)} %param.19) | copy-start | bytes 393220
  6.5 5.0 %copy-start.8 = (f32[2]{0:T(128)S(1)}, f32[2]{0:T(128)}, u32[]{:S(2)}) copy-start(f32[2]{0:T(128)} %param.14) | copy-start | bytes 28
  6.5 5.0 %copy-start.3 = (s32[16,256]{1,0:T(8,128)S(1)}, s32[16,256]{1,0:T(8,128)}, u32[]{:S(2)}) copy-start(s32[16,256]{1,0:T(8,128)} %param.16) | copy-start | bytes 49156
  6.5 145.8 %all-gather.2.cloned.1.call-start = ((), (), s32[]{:S(2)}) async-start(), calls=%async_computation | async-start | bytes 3244032 | tf_op jit(solution)/shard_map/all_gather | solution.py:83
  11.5 206.3 %all-reduce.3.cloned.1.call-start = ((), (), s32[]{:S(2)}) async-start(), calls=%async_computation.1 | async-start | bytes 393216 | tf_op jit(solution)/shard_map/psum | solution.py:102
  157.0 2.6 copy-start.6
  159.7 3.3 %copy-start.2 = (bf16[7,7,256]{2,1,0:T(8,128)(2,1)S(1)}, bf16[7,7,256]{2,1,0:T(8,128)(2,1)}, u32[]{:S(2)}) copy-start(bf16[7,7,256]{2,1,0:T(8,128)(2,1)} %param.17) | copy-start | bytes 75268
  159.7 58.2 %copy-start.1 = (bf16[16,24,256]{2,1,0:T(8,128)(2,1)S(1)}, bf16[16,24,256]{2,1,0:T(8,128)(2,1)}, u32[]{:S(2)}) copy-start(bf16[16,24,256]{2,1,0:T(8,128)(2,1)} %param.11) | copy-start | bytes 589828
  162.9 138.5 %all-reduce.5.cloned.1.call-start = ((), (), s32[]{:S(2)}) async-start(), calls=%async_computation.2 | async-start | bytes 393216 | tf_op jit(solution)/shard_map/psum | solution.py:108
  218.8 2.6 collective-permute-start
  220.1 5.4 %collective-permute-start.1 = (bf16[3,24,256]{2,1,0:T(8,128)(2,1)S(1)}, bf16[3,24,256]{2,1,0:T(8,128)(2,1)S(1)}, u32[]{:S(2)}, u32[]{:S(2)}) collective-permute-start(bf16[3,24,256]{2,1,0:T(8,128)(2,1)S(1)} %get-tuple-element.12), channel_id=1, source_target_pairs={{128,0},{256,128},{384,256},{129,1},{257,129},{385,257},{130,2},{2... | collective-permute-start | bytes 110600 | tf_op jit(solution)/shard_map/ppermute | solution.py:19
  225.6 6.3 %collective-permute-start.2 = (bf16[22,3,256]{2,1,0:T(4,128)(2,1)S(1)}, bf16[22,3,256]{2,1,0:T(4,128)(2,1)S(1)}, u32[]{:S(2)}, u32[]{:S(2)}) collective-permute-start(bf16[22,3,256]{2,1,0:T(4,128)(2,1)S(1)} %get-tuple-element.9), channel_id=1, source_target_pairs={{0,4},{4,8},{8,12},{12,16},{16,20},{20,24},{24,28},{28,32},{32,36}... | collective-permute-start | bytes 101384 | tf_op jit(solution)/shard_map/ppermute | solution.py:18
  230.0 6.8 %collective-permute-start.3 = (bf16[22,3,256]{2,1,0:T(4,128)(2,1)S(1)}, bf16[22,3,256]{2,1,0:T(4,128)(2,1)S(1)}, u32[]{:S(2)}, u32[]{:S(2)}) collective-permute-start(bf16[22,3,256]{2,1,0:T(4,128)(2,1)S(1)} %get-tuple-element.10), channel_id=1, source_target_pairs={{4,0},{8,4},{12,8},{16,12},{20,16},{24,20},{28,24},{32,28},{36,32}... | collective-permute-start | bytes 101384 | tf_op jit(solution)/shard_map/ppermute | solution.py:19
  236.9 3.2 %copy-start.7 = (f32[256]{0:T(256)S(1)}, f32[256]{0:T(256)}, u32[]{:S(2)}) copy-start(f32[256]{0:T(256)} %param.18) | copy-start | bytes 3076
  237.0 3.6 %copy-start.5 = (bf16[256,256]{1,0:T(8,128)(2,1)S(1)}, bf16[256,256]{1,0:T(8,128)(2,1)}, u32[]{:S(2)}) copy-start(bf16[256,256]{1,0:T(8,128)(2,1)} %param.20) | copy-start | bytes 393220
  240.5 1.8 copy-start.4
Sparse Core Ops, SparseCore 0:
  11.6 140.6 all-gather.1
  163.0 54.7 all-reduce.2
  242.4 58.8 all-reduce.4
where the time goes:
time: 310 us
  waiting for transfers between devices  264 us (85%)
  between operations  13.4 us (4%)
  starting transfers between devices  8.95 us (3%)
  other arithmetic  8.84 us (3%)
  matrix products  8.69 us (3%)
  local copies, waits for them, and re-layouts  6.01 us (2%)
    all_gather x1, waiting for transfers between devices, shards(): piece = lax.all_gather(keys_values, 'lon', axis=1, tiled=True)  141 us
    psum x1, waiting for transfers between devices, shards(): lax.psum(feed_forward(spatial, norm_gain2, w_up, w_down).astype(jnp.bfloa...  59 us
    psum x1, waiting for transfers between devices, shards(): lax.psum(partial_value.astype(jnp.bfloat16), 'tensor').astype(jnp.float32)  54.8 us
    ppermute x2, waiting for transfers between devices, padded(): after = lax.ppermute(first, axis, down)  8.96 us
  transfers between devices with their start and end apart: 7, of which 5 were waited for; matrix products, arithmetic and copies ran while one was open for 0% of the time, Pallas kernels for 0%

commit v1 on v0

--- a/solution.py
+++ b/solution.py
@@ -80,7 +80,9 @@
     ).astype(jnp.bfloat16)
     queries = projected[:, :, 0]
     keys_values = projected[:, :, 1:].reshape(lat_rows, lon_cols, 2 * local_heads * head_size)
-    piece = lax.all_gather(keys_values, "lon", axis=1, tiled=True)
+    piece = jnp.concatenate(
+        lax.all_to_all(jnp.stack([keys_values] * lax.axis_size("lon")), "lon", 0, 0), axis=1
+    )
     running_max = jnp.full((lat_rows, local_heads, lon_cols), -1e30, jnp.float32)
     count = piece.shape[1]
     split_piece = piece.reshape(lat_rows, count, 2, local_heads, head_size)

time: 310 us -> 393 us (1.27)
  local copies, waits for them, and re-layouts: 6.01 us -> 73.5 us
  starting transfers between devices: 8.95 us -> 25.8 us
    all_to_all x0 -> x1, waiting for transfers between devices: none -> 145 us  [shards(): lax.all_to_all(jnp.stack([keys_values] * lax.axis_size('lon')), 'lon', 0, 0)]
    all_gather x1 -> x0, waiting for transfers between devices: 141 us -> none  [shards(): piece = lax.all_gather(keys_values, 'lon', axis=1, tiled=True)]
    unnamed x18 -> x22, local copies, waits for them, and re-layouts: 0.05 us -> 30.8 us
    another operation x0 -> x3, local copies, waits for them, and re-layouts: none -> 28.1 us  [the longest x1 25.6 us: shards(): split_piece = piece.reshape(lat_rows, count, 2, local_heads, head_size)]
    all_to_all x0 -> x1, starting transfers between devices: none -> 16.8 us  [shards(): lax.all_to_all(jnp.stack([keys_values] * lax.axis_size('lon')), 'lon', 0, 0)]
    slice x0 -> x1, local copies, waits for them, and re-layouts: none -> 11.6 us  [shards(): split_piece[:, :, 0]]
    psum x1, waiting for transfers between devices: 54.8 us -> 48.1 us  [shards(): lax.psum(partial_value.astype(jnp.bfloat16), 'tensor').astype(jnp.float32)]
    all_gather x1 -> x0, local copies, waits for them, and re-layouts: 4.69 us -> none  [shards(): piece = lax.all_gather(keys_values, 'lon', axis=1, tiled=True)]
where the time goes in v1:
time: 393 us; the launch traced here: 392 us
  waiting for transfers between devices  261 us (66%)
  local copies, waits for them, and re-layouts  73.5 us (19%)
  starting transfers between devices  25.8 us (7%)
  between operations  13.7 us (3%)
  other arithmetic  8.84 us (2%)
  matrix products  8.79 us (2%)
    all_to_all x1, waiting for transfers between devices, shards(): lax.all_to_all(jnp.stack([keys_values] * lax.axis_size('lon')), 'lon', 0, 0)  145 us
    psum x1, waiting for transfers between devices, shards(): lax.psum(feed_forward(spatial, norm_gain2, w_up, w_down).astype(jnp.bfloa...  59 us
    psum x1, waiting for transfers between devices, shards(): lax.psum(partial_value.astype(jnp.bfloat16), 'tensor').astype(jnp.float32)  48.1 us
    unnamed x22, local copies, waits for them, and re-layouts  30.8 us
    another operation x1, local copies, waits for them, and re-layouts, shards(): split_piece = piece.reshape(lat_rows, count, 2, local_heads, head_size)  25.6 us
    all_to_all x1, starting transfers between devices, shards(): lax.all_to_all(jnp.stack([keys_values] * lax.axis_size('lon')), 'lon', 0, 0)  16.8 us
    slice x1, local copies, waits for them, and re-layouts, shards(): split_piece[:, :, 0]  11.6 us
    ppermute x2, waiting for transfers between devices, padded(): after = lax.ppermute(first, axis, down)  8.96 us
  transfers between devices with their start and end apart: 7, of which 5 were waited for; matrix products, arithmetic and copies ran while one was open for 0% of the time, Pallas kernels for 0%

profile of v1, /device:TPU:2, one launch (start us, length us, event | category | flops | bytes accessed | tf_op | source)
XLA Modules:
  0.0 391.9 jit_solution(2880584676956770868)
XLA Ops:
  6.5 1.1 convert_reduce_fusion
  7.6 1.2 fusion.26
  8.8 1.4 convolution_convert_fusion
  10.2 0.9 copy-done.2
  11.2 0.3 copy.14
  11.5 0.2 stack_reshape.2
  11.7 2.4 stack.3
  14.1 16.8 %all-to-all-start = ((bf16[32,16,24,128]{3,2,1,0:T(8,128)(2,1)}), bf16[32,16,24,128]{3,2,1,0:T(8,128)(2,1)S(1)}, u32[]{:S(2)}, u32[]{:S(2)}) async-start(bf16[32,16,24,128]{3,2,1,0:T(8,128)(2,1)} %stack.3), calls=%async_computation | async-start | bytes 6291456 | tf_op jit(solution)/shard_map/all_to_all | solution.py:84
  31.0 145.2 %all-to-all-done = bf16[32,16,24,128]{3,2,1,0:T(8,128)(2,1)S(1)} async-done(((bf16[32,16,24,128]{3,2,1,0:T(8,128)(2,1)}), bf16[32,16,24,128]{3,2,1,0:T(8,128)(2,1)S(1)}, u32[]{:S(2)}, u32[]{:S(2)}) %all-to-all-start) | async-done | bytes 3145760 | tf_op jit(solution)/shard_map/all_to_all | solution.py:84
  176.2 2.5 copy.15
  178.7 25.6 %reshape_reshape.3 = bf16[16,768,2,2,32]{4,3,2,1,0:T(2,128)(2,1)} reshape(bf16[16,32,24,128]{3,2,1,0:T(8,128)(2,1)} %copy.15) | data formatting | bytes 6291456 | tf_op jit(solution)/shard_map/reshape;reshape | solution.py:88
  204.2 11.6 %fusion.143 = (bf16[16,768,1,2,32]{4,3,2,1,0:T(2,128)(2,1)}, bf16[16,768,1,2,32]{4,3,2,1,0:T(2,128)(2,1)}) fusion(bf16[16,768,2,2,32]{4,3,2,1,0:T(2,128)(2,1)} %reshape_reshape.3), kind=kLoop, calls=%fused_computation.214 | loop fusion | bytes 6291456 | tf_op jit(solution)/shard_map/slice | solution.py:90
  215.8 14.9 %copy.20 = bf16[16,768,1,2,32]{1,4,3,0,2:T(8,128)(2,1)} copy(bf16[16,768,1,2,32]{4,3,2,1,0:T(2,128)(2,1)} %get-tuple-element.9) | data formatting | bytes 3145728
  230.7 2.1 multiply_reduce_fusion
  232.8 14.9 %copy.21 = bf16[16,768,1,2,32]{1,4,3,0,2:T(8,128)(2,1)} copy(bf16[16,768,1,2,32]{4,3,2,1,0:T(2,128)(2,1)} %get-tuple-element.10) | data formatting | bytes 3145728
  247.7 0.6 fusion
  248.3 0.2 copy-done.7
  248.5 3.2 fusion.17
  251.8 48.1 %all-reduce.3.cloned.1.call-done = bf16[16,24,256]{2,1,0:T(8,128)(2,1)} async-done(((bf16[16,24,256]{2,1,0:T(8,128)(2,1)}), bf16[16,24,256]{2,1,0:T(8,128)(2,1)}) %all-reduce.3.cloned.1.call-update) | async-done | bytes 196624 | tf_op jit(solution)/shard_map/psum | solution.py:104
  299.9 1.0 fusion.32
  300.9 1.3 collective-permute-start
  302.2 1.3 collective-permute-start.1
  303.5 4.1 %collective-permute-done.1 = bf16[3,24,256]{2,1,0:T(8,128)(2,1)S(1)} collective-permute-done((bf16[3,24,256]{2,1,0:T(8,128)(2,1)S(1)}, bf16[3,24,256]{2,1,0:T(8,128)(2,1)S(1)}, u32[]{:S(2)}, u32[]{:S(2)}) %collective-permute-start.1) | collective-permute-done | bytes 36896 | tf_op jit(solution)/shard_map/ppermute | solution.py:19
  307.7 4.4 %collective-permute-start.2 = (bf16[22,3,256]{2,1,0:T(4,128)(2,1)S(1)}, bf16[22,3,256]{2,1,0:T(4,128)(2,1)S(1)}, u32[]{:S(2)}, u32[]{:S(2)}) collective-permute-start(bf16[22,3,256]{2,1,0:T(4,128)(2,1)S(1)} %get-tuple-element.11), channel_id=1, source_target_pairs={{0,4},{4,8},{8,12},{12,16},{16,20},{20,24},{24,28},{28,32},{32,36}... | collective-permute-start | bytes 101384 | tf_op jit(solution)/shard_map/ppermute | solution.py:18
  312.0 1.9 collective-permute-start.3
  314.0 4.9 %collective-permute-done.3 = bf16[22,3,256]{2,1,0:T(4,128)(2,1)S(1)} collective-permute-done((bf16[22,3,256]{2,1,0:T(4,128)(2,1)S(1)}, bf16[22,3,256]{2,1,0:T(4,128)(2,1)S(1)}, u32[]{:S(2)}, u32[]{:S(2)}) %collective-permute-start.3) | collective-permute-done | bytes 33824 | tf_op jit(solution)/shard_map/ppermute | solution.py:19
  319.0 2.9 convert_reduce_fusion.1
  322.0 0.2 fusion.29
  322.2 0.3 fusion.103
  322.6 1.8 convolution_convert_fusion.1
  324.4 59.0 %all-reduce.5.cloned.1.call-done = bf16[16,24,256]{2,1,0:T(8,128)(2,1)} async-done(((bf16[16,24,256]{2,1,0:T(8,128)(2,1)}), bf16[16,24,256]{2,1,0:T(8,128)(2,1)}) %all-reduce.5.cloned.1.call-update) | async-done | bytes 196624 | tf_op jit(solution)/shard_map/psum | solution.py:110
  383.4 1.7 add_convert_fusion
  (39 shorter events, 0.5 us)
Async XLA Ops:
  6.5 315.7 %copy-start = (bf16[256,256]{1,0:T(8,128)(2,1)S(1)}, bf16[256,256]{1,0:T(8,128)(2,1)}, u32[]{:S(2)}) copy-start(bf16[256,256]{1,0:T(8,128)(2,1)} %param.19) | copy-start | bytes 393220
  10.2 0.9 copy-start.2
  14.1 16.9 %copy-start.9 = (f32[2]{0:T(128)S(1)}, f32[2]{0:T(128)}, u32[]{:S(2)}) copy-start(f32[2]{0:T(128)} %param.14) | copy-start | bytes 28
  14.1 16.9 %copy-start.4 = (s32[16,256]{1,0:T(8,128)S(1)}, s32[16,256]{1,0:T(8,128)}, u32[]{:S(2)}) copy-start(s32[16,256]{1,0:T(8,128)} %param.16) | copy-start | bytes 49156
  14.1 162.1 %all-to-all-start = ((bf16[32,16,24,128]{3,2,1,0:T(8,128)(2,1)}), bf16[32,16,24,128]{3,2,1,0:T(8,128)(2,1)S(1)}, u32[]{:S(2)}, u32[]{:S(2)}) async-start(bf16[32,16,24,128]{3,2,1,0:T(8,128)(2,1)} %stack.3), calls=%async_computation | async-start | bytes 6291456 | tf_op jit(solution)/shard_map/all_to_all | solution.py:84
  30.9 269.0 %all-reduce.3.cloned.1.call-start = ((), (), s32[]{:S(2)}) async-start(), calls=%async_computation.1 | async-start | bytes 393216 | tf_op jit(solution)/shard_map/psum | solution.py:104
  247.7 0.8 copy-start.7
  248.5 3.3 copy-start.3
  248.5 51.4 %copy-start.1 = (bf16[16,24,256]{2,1,0:T(8,128)(2,1)S(1)}, bf16[16,24,256]{2,1,0:T(8,128)(2,1)}, u32[]{:S(2)}) copy-start(bf16[16,24,256]{2,1,0:T(8,128)(2,1)} %param.11) | copy-start | bytes 589828
  251.7 131.7 %all-reduce.5.cloned.1.call-start = ((), (), s32[]{:S(2)}) async-start(), calls=%async_computation.2 | async-start | bytes 393216 | tf_op jit(solution)/shard_map/psum | solution.py:110
  300.9 2.6 collective-permute-start
  302.2 5.4 %collective-permute-start.1 = (bf16[3,24,256]{2,1,0:T(8,128)(2,1)S(1)}, bf16[3,24,256]{2,1,0:T(8,128)(2,1)S(1)}, u32[]{:S(2)}, u32[]{:S(2)}) collective-permute-start(bf16[3,24,256]{2,1,0:T(8,128)(2,1)S(1)} %get-tuple-element.14), channel_id=1, source_target_pairs={{128,0},{256,128},{384,256},{129,1},{257,129},{385,257},{130,2},{2... | collective-permute-start | bytes 110600 | tf_op jit(solution)/shard_map/ppermute | solution.py:19
  307.7 6.3 %collective-permute-start.2 = (bf16[22,3,256]{2,1,0:T(4,128)(2,1)S(1)}, bf16[22,3,256]{2,1,0:T(4,128)(2,1)S(1)}, u32[]{:S(2)}, u32[]{:S(2)}) collective-permute-start(bf16[22,3,256]{2,1,0:T(4,128)(2,1)S(1)} %get-tuple-element.11), channel_id=1, source_target_pairs={{0,4},{4,8},{8,12},{12,16},{16,20},{20,24},{24,28},{28,32},{32,36}... | collective-permute-start | bytes 101384 | tf_op jit(solution)/shard_map/ppermute | solution.py:18
  312.0 6.8 %collective-permute-start.3 = (bf16[22,3,256]{2,1,0:T(4,128)(2,1)S(1)}, bf16[22,3,256]{2,1,0:T(4,128)(2,1)S(1)}, u32[]{:S(2)}, u32[]{:S(2)}) collective-permute-start(bf16[22,3,256]{2,1,0:T(4,128)(2,1)S(1)} %get-tuple-element.12), channel_id=1, source_target_pairs={{4,0},{8,4},{12,8},{16,12},{20,16},{24,20},{28,24},{32,28},{36,32}... | collective-permute-start | bytes 101384 | tf_op jit(solution)/shard_map/ppermute | solution.py:19
  319.0 3.2 copy-start.8
  319.0 3.6 copy-start.6
  322.6 1.8 copy-start.5
Sparse Core Ops, SparseCore 0:
  251.8 48.0 all-reduce.2
  324.5 58.8 all-reduce.4
